TPU v7x, 32 devices: a whole 2x2x4 slice. The times are simulated.
32 devices in a mesh: px: 16 (over z, x, core), py: 2 (over y).
Axes of the slice: x: 2, y: 2, z: 4, core: 2. Of those that a mesh axis runs over, the one named last changes fastest.
Arguments:
- latents: float32 [32, 4, 128, 512], P('px', 'py'), may hold values from -6 to 6
- cotangent: float32 [32, 4, 128, 512], P('px', 'py'), may hold values from -6 to 6
- w_src: bfloat16 [512, 512], replicated, may hold values from -0.25 to 0.25
- w_dst: bfloat16 [512, 512], replicated, may hold values from -0.25 to 0.25
- b_edge: float32 [512], replicated, may hold values from -3 to 3
- w_msg: bfloat16 [512, 512], replicated, may hold values from -0.25 to 0.25
- w_self: bfloat16 [512, 512], replicated, may hold values from -0.25 to 0.25
- w_agg: bfloat16 [512, 512], replicated, may hold values from -0.25 to 0.25
- b_node: float32 [512], replicated, may hold values from -3 to 3
- w_out: bfloat16 [512, 512], replicated, may hold values from -0.25 to 0.25
- src_block: int32 [16, 2, 12], P('px', 'py'), may hold values from 0 to 11
- dst_block: int32 [16, 2, 12], P('px', 'py'), may hold values from 0 to 3
- src_node: int32 [16, 2, 12, 128], P('px', 'py'), may hold values from 0 to 127
- dst_node: int32 [16, 2, 12, 128], P('px', 'py'), may hold values from 0 to 127
- long_src: int32 [16, 2, 512], P('px', 'py'), may hold values from 0 to 511, as said below
- long_dst: int32 [16, 2, 512], P('px', 'py'), may hold values from 0 to 511
Outputs:
- grad_latents: float32 [32, 4, 128, 512], P('px', 'py')
- grad_w_src: float32 [512, 512], replicated
- grad_w_dst: float32 [512, 512], replicated
- grad_b_edge: float32 [512], replicated
- grad_w_msg: float32 [512, 512], replicated
- grad_w_self: float32 [512, 512], replicated
- grad_w_agg: float32 [512, 512], replicated
- grad_b_node: float32 [512], replicated
- grad_w_out: float32 [512, 512], replicated
Inputs may be any that keep to these rules, and one draw needn't show every extreme that they name: `long_src`: the coarse edges of one patch come from the coarse nodes of any one patch at most 32 times; in every draw one patch is named exactly 32 times by every patch.
All inputs are finite; a program needn't handle non-finite values.
Results may differ from a plain program's by a relative error of at most 0.011.
Values may be sent and summed in bfloat16 or wider, within the bound.
A program may use at most 128 MiB of HBM per device.

v0:
```python
import jax
import jax.numpy as jnp
from jax import lax
from jax.sharding import PartitionSpec as P

C_DEV = 16


def shifted(shard, axis, by):
    size = lax.axis_size(axis)
    return lax.ppermute(shard, axis, [(i, (i + by) % size) for i in range(size)])


def shifted_2(block, axis, distance):
    devices = range(lax.axis_size(axis))
    route = [(i - distance, i) for i in devices if i - distance in devices]
    return lax.ppermute(block, axis, route)


def padded(block, sides, width, periodic):
    for axis, dim in sides:
        count = lax.axis_size(axis)
        forward = [(i, i + 1) for i in range(count - 1)]
        if periodic:
            forward.append((count - 1, 0))
        backward = [(target, source) for source, target in forward]
        low = lax.ppermute(
            lax.slice_in_dim(block, block.shape[dim] - width, None, axis=dim), axis, forward
        )
        high = lax.ppermute(lax.slice_in_dim(block, 0, width, axis=dim), axis, backward)
        block = jnp.concatenate([low, block, high], axis=dim)
    return block


def product(left, right):
    return jnp.dot(left, right, preferred_element_type=jnp.float32)


def silu_slope(value):
    sigma = jax.nn.sigmoid(value)
    return sigma * (1.0 + value * (1.0 - sigma))


def return_lon(value, step):
    return shifted(value, "px", step)


def return_lat(value, step):
    return shifted_2(value.astype(jnp.bfloat16), "py", step).astype(value.dtype)


def body(
    latents,
    cotangent,
    w_src,
    w_dst,
    b_edge,
    w_msg,
    w_self,
    w_agg,
    b_node,
    w_out,
    src_block,
    dst_block,
    src_node,
    dst_node,
    long_src,
    long_dst,
):
    rows_x, rows_y, block, width = latents.shape
    inner = rows_x * rows_y
    local_nodes = inner * block
    tiles = src_block.shape[-1]
    long_count = long_src.shape[-1]
    fine_count = tiles * block
    highest = lax.Precision.HIGHEST
    rounded = latents.astype(jnp.bfloat16)
    own_blocks = rounded.reshape(inner, block, width)
    own_rows = rounded.reshape(local_nodes, width)
    along_px = padded(rounded, (("px", 0),), 1, True)
    along_py = padded(rounded, (("py", 1),), 1, False)
    table = jnp.concatenate(
        [own_blocks, along_px[0], along_px[rows_x + 1], along_py[:, 0], along_py[:, rows_y + 1]],
        axis=0,
    )
    slot_count = table.shape[0]
    src_slots = src_block.reshape(tiles)
    dst_slots = dst_block.reshape(tiles)
    src_nodes = src_node.reshape(tiles, block)
    dst_nodes = dst_node.reshape(tiles, block)
    long_from = long_src.reshape(long_count)
    long_into = long_dst.reshape(long_count)
    node_ids = jnp.arange(block, dtype=jnp.int32)
    src_onehot = (src_nodes[:, :, None] == node_ids).astype(jnp.bfloat16)
    dst_onehot = (dst_nodes[:, :, None] == node_ids).astype(jnp.bfloat16)
    slot_pick = (src_slots[:, None] == jnp.arange(slot_count, dtype=jnp.int32)).astype(jnp.float32)
    block_pick = (dst_slots[:, None] == jnp.arange(inner, dtype=jnp.int32)).astype(jnp.float32)
    long_onehot = (long_into[:, None] == jnp.arange(local_nodes, dtype=jnp.int32)).astype(
        jnp.bfloat16
    )
    src_tiles = jnp.take(table, src_slots, axis=0)
    fine_src = jnp.einsum(
        "fen,fnd->fed", src_onehot, src_tiles, preferred_element_type=jnp.float32
    ).astype(jnp.bfloat16)
    dst_tiles = jnp.take(own_blocks, dst_slots, axis=0)
    fine_dst = jnp.einsum(
        "fen,fnd->fed", dst_onehot, dst_tiles, preferred_element_type=jnp.float32
    ).astype(jnp.bfloat16)
    stride = local_nodes // C_DEV
    coarse_rows = own_rows[::stride]
    piece = lax.all_gather(coarse_rows, ("px", "py"), axis=0, tiled=True)
    offset = long_from
    inside = (offset >= 0) & (offset < piece.shape[0])
    chosen = jnp.take(piece, jnp.clip(offset, 0, piece.shape[0] - 1), axis=0)
    long_sender = jnp.where(inside[:, None], chosen.astype(jnp.float32), 0.0)
    long_sender = long_sender.astype(jnp.bfloat16)
    long_receiver = product(long_onehot, own_rows).astype(jnp.bfloat16)
    sender = jnp.concatenate([fine_src.reshape(fine_count, width), long_sender], axis=0)
    receiver = jnp.concatenate([fine_dst.reshape(fine_count, width), long_receiver], axis=0)
    pre_edge = product(sender, w_src) + product(receiver, w_dst) + b_edge
    edge_act = jax.nn.silu(pre_edge).astype(jnp.bfloat16)
    message = product(edge_act, w_msg).astype(jnp.bfloat16)
    per_tile = jnp.einsum(
        "fen,fed->fnd",
        dst_onehot,
        message[:fine_count].reshape(tiles, block, width),
        preferred_element_type=jnp.float32,
    )
    incoming = jnp.einsum("fb,fnd->bnd", block_pick, per_tile, precision=highest).reshape(
        local_nodes, width
    )
    incoming = incoming + jnp.einsum(
        "en,ed->nd", long_onehot, message[fine_count:], preferred_element_type=jnp.float32
    )
    incoming_b = incoming.astype(jnp.bfloat16)
    node_pre = product(own_rows, w_self) + product(incoming_b, w_agg) + b_node
    node_act = jax.nn.silu(node_pre).astype(jnp.bfloat16)
    cot_b = cotangent.reshape(local_nodes, width).astype(jnp.bfloat16)
    d_out = product(node_act.T, cot_b)
    g_node = (product(cot_b, w_out.T) * silu_slope(node_pre)).astype(jnp.bfloat16)
    d_self = product(own_rows.T, g_node)
    d_agg = product(incoming_b.T, g_node)
    d_bnode = jnp.sum(g_node.astype(jnp.float32), axis=0)
    g_self = product(g_node, w_self.T)
    g_incoming = product(g_node, w_agg.T).astype(jnp.bfloat16)
    incoming_tiles = jnp.take(g_incoming.reshape(inner, block, width), dst_slots, axis=0)
    fine_gmsg = jnp.einsum(
        "fen,fnd->fed", dst_onehot, incoming_tiles, preferred_element_type=jnp.float32
    ).astype(jnp.bfloat16)
    long_gmsg = product(long_onehot, g_incoming).astype(jnp.bfloat16)
    g_message = jnp.concatenate([fine_gmsg.reshape(fine_count, width), long_gmsg], axis=0)
    d_msg = product(edge_act.T, g_message)
    g_pre = (product(g_message, w_msg.T) * silu_slope(pre_edge)).astype(jnp.bfloat16)
    d_src = product(sender.T, g_pre)
    d_dst = product(receiver.T, g_pre)
    d_bedge = jnp.sum(g_pre.astype(jnp.float32), axis=0)
    g_send = product(g_pre, w_src.T).astype(jnp.bfloat16)
    g_recv = product(g_pre, w_dst.T).astype(jnp.bfloat16)
    send_tiles = jnp.einsum(
        "fen,fed->fnd",
        src_onehot,
        g_send[:fine_count].reshape(tiles, block, width),
        preferred_element_type=jnp.float32,
    )
    slot_grads = jnp.einsum("fs,fnd->snd", slot_pick, send_tiles, precision=highest)
    recv_tiles = jnp.einsum(
        "fen,fed->fnd",
        dst_onehot,
        g_recv[:fine_count].reshape(tiles, block, width),
        preferred_element_type=jnp.float32,
    )
    edge_grad = (
        jnp.einsum("fb,fnd->bnd", block_pick, recv_tiles, precision=highest) + slot_grads[:inner]
    )
    edge_grad = edge_grad.reshape(local_nodes, width)
    edge_grad = edge_grad + jnp.einsum(
        "en,ed->nd", long_onehot, g_recv[fine_count:], preferred_element_type=jnp.float32
    )
    top_rim = slot_grads[inner : inner + rows_y]
    bottom_rim = slot_grads[inner + rows_y : inner + 2 * rows_y]
    left_rim = slot_grads[inner + 2 * rows_y : inner + 2 * rows_y + rows_x]
    right_rim = slot_grads[inner + 2 * rows_y + rows_x :]
    from_next = return_lon(top_rim, -1)
    from_prior = return_lon(bottom_rim, 1)
    from_right = return_lat(left_rim, -1)
    from_left = return_lat(right_rim, 1)
    grid = edge_grad.reshape(rows_x, rows_y, block, width)
    grid = grid.at[rows_x - 1].add(from_next)
    grid = grid.at[0].add(from_prior)
    grid = grid.at[:, rows_y - 1].add(from_right)
    grid = grid.at[:, 0].add(from_left)
    long_grad = g_send[fine_count:].astype(jnp.float32)
    coarse_count = coarse_rows.shape[0]
    count = coarse_count * lax.axis_size(("px", "py"))
    offset = long_from
    inside = (offset >= 0) & (offset < count)
    segment = jnp.where(inside, offset, count)
    coarse_grad = lax.psum_scatter(
        jax.ops.segment_sum(long_grad, segment, num_segments=count + 1)[:count],
        ("px", "py"),
        scatter_dimension=0,
        tiled=True,
    )
    flat_grad = grid.reshape(local_nodes, width).at[::stride].add(coarse_grad)
    grad_latents = (cotangent.reshape(local_nodes, width) + g_self + flat_grad).reshape(
        rows_x, rows_y, block, width
    )
    d_src, d_dst, d_bedge, d_msg, d_self, d_agg, d_bnode, d_out = lax.psum(
        (d_src, d_dst, d_bedge, d_msg, d_self, d_agg, d_bnode, d_out), ("px", "py")
    )
    return (grad_latents, d_src, d_dst, d_bedge, d_msg, d_self, d_agg, d_bnode, d_out)


def solution(mesh):
    in_specs = (
        P("px", "py", None, None),
        P("px", "py", None, None),
        P(),
        P(),
        P(),
        P(),
        P(),
        P(),
        P(),
        P(),
        P("px", "py", None),
        P("px", "py", None),
        P("px", "py", None, None),
        P("px", "py", None, None),
        P("px", "py", None),
        P("px", "py", None),
    )
    out_specs = (P("px", "py", None, None), P(), P(), P(), P(), P(), P(), P(), P())
    return jax.shard_map(body, mesh=mesh, in_specs=in_specs, out_specs=out_specs, check_vma=False)
```

profile of v0, /device:TPU:0, one launch (start us, length us, event | category | flops | bytes accessed | tf_op | source)
XLA Modules:
  0.0 457.6 jit_solution(16048870041952088093)
XLA Ops:
  7.3 1.3 convert_element_type.73
  8.6 0.8 fusion.70
  9.5 5.4 %collective-permute-start.1 = (bf16[1,2,128,512]{3,2,1,0:T(8,128)(2,1)}, bf16[1,2,128,512]{3,2,1,0:T(8,128)(2,1)}, u32[]{:S(2)}, u32[]{:S(2)}) collective-permute-start(bf16[1,2,128,512]{3,2,1,0:T(8,128)(2,1)} %get-tuple-element.90), channel_id=1, source_target_pairs={{2,0},{4,2},{6,4},{8,6},{10,8},{12,10},{14,12},{16,14},{18,16},{20... | collective-permute-start | bytes 786440 | tf_op jit(solution)/shard_map/ppermute | solution.py:30
  14.9 0.8 fusion.69
  15.8 1.4 collective-permute-start.3
  17.2 5.3 %collective-permute-start.2 = (bf16[2,1,128,512]{3,2,1,0:T(8,128)(2,1)}, bf16[2,1,128,512]{3,2,1,0:T(8,128)(2,1)}, u32[]{:S(2)}, u32[]{:S(2)}) collective-permute-start(bf16[2,1,128,512]{3,2,1,0:T(8,128)(2,1)} %get-tuple-element.89), channel_id=1, source_target_pairs={{0,1},{2,3},{4,5},{6,7},{8,9},{10,11},{12,13},{14,15},{16,17},{18,... | collective-permute-start | bytes 786440 | tf_op jit(solution)/shard_map/ppermute | solution.py:27
  22.7 68.7 %all_gather.3 = bf16[512,512]{1,0:T(8,128)(2,1)S(1)} all-gather(bf16[16,512]{1,0:T(8,128)(2,1)S(1)} %slice.166), channel_id=1, replica_groups=mesh['px'=16,'py'=2] {'px','py'}, dimensions={0}, use_global_device_ids=true | all-gather | bytes 540672 | tf_op jit(solution)/shard_map/all_gather | solution.py:111
  91.4 1.3 convolution_convert_fusion.8
  92.7 0.8 bitcast_convert_fusion
  93.5 1.4 fusion.72
  94.9 2.0 gather_fusion.1
  96.9 0.6 gather_fusion.2
  97.6 1.0 select_convert_fusion
  98.6 1.8 convolution_convert_fusion.4
  100.4 0.8 constant_dynamic-update-slice_fusion
  101.2 1.7 bitcast_dynamic-update-slice_fusion.3
  102.9 1.7 bitcast_dynamic-update-slice_fusion.2
  104.6 1.7 bitcast_dynamic-update-slice_fusion.1
  106.2 0.7 bitcast_dynamic-update-slice_fusion
  107.0 2.1 gather_fusion
  110.2 1.2 fusion.20
  111.8 4.5 multiply_convert_fusion.1
  116.3 1.2 convolution_convert_fusion.2
  117.7 1.6 fusion.30
  119.3 3.2 fusion.4
  125.1 0.7 convert_reduce_fusion.1
  126.6 1.4 fusion.73
  128.5 1.9 gather_fusion.3
  130.4 2.0 convolution_convert_fusion.3
  132.5 5.8 %convert_reduce_fusion = (f32[512]{0:T(512)S(1)}, bf16[2048,512]{1,0:T(8,128)(2,1)S(1)}) fusion(f32[2048,512]{1,0:T(8,128)} %get-tuple-element.95, bf16[512,512]{1,0:T(8,128)(2,1)S(1)} %copy-done.36, bf16[512,512]{1,0:T(8,128)(2,1)S(1)} %convolution_convert_fusion.6, bf16[1536,512]{1,0:T(8,128)(2,1)S(1)} %bitcast.122), kind=kOutput, calls=%fused_computation.12 | convolution fusion | flops 1089469952 | bytes 8914944 | tf_op jit(solution)/shard_map/dot_general | solution.py:36
  138.3 1.3 convolution_convert_fusion
  139.6 2.6 convolution_convert_fusion.1
  142.2 4.4 scatter_custom_fusion
  146.6 1.0 slice.210
  147.8 2.8 slice.197
  150.6 1.4 convolution_bitcast_fusion
  152.1 1.5 fusion.41
  153.6 1.6 fusion.28
  155.8 2.2 fusion.17
  158.1 2.2 fusion.18
  160.3 2.2 fusion.19
  162.6 2.4 fusion.29
  165.0 4.0 fusion.71
  169.0 3.4 fusion.12
  173.3 0.9 copy.41
  174.2 0.7 collective-permute-start.5
  175.0 1.2 fusion.68
  176.1 1.6 collective-permute-start.7
  177.7 1.3 collective-permute-start.6
  179.0 1.6 convolution_add_fusion
  180.7 0.8 copy.32
  181.5 39.5 %all-reduce = (f32[512]{0:T(512)}, f32[512]{0:T(512)}) all-reduce(f32[512]{0:T(512)S(1)} %get-tuple-element.98, f32[512]{0:T(512)S(1)} %get-tuple-element.100), channel_id=1, replica_groups=mesh['px'=16,'py'=2] {'px','py'}, use_global_device_ids=true, to_apply=%region_6.8 | all-reduce | flops 1024 | bytes 8192 | tf_op jit(solution)/shard_map/psum | solution.py:208
  221.5 4.8 %scatter-add.26 = f32[2,2,128,512]{3,0,2,1:T(2,128)S(1)} dynamic-update-slice(f32[2,2,128,512]{3,0,2,1:T(2,128)S(1)} %copy.32, f32[1,2,128,512]{3,0,2,1:T(1,128)S(1)} %add.161, s32[]{:T(128)} %constant.160.clone.1, s32[]{:T(128)} %constant.153.clone.1, s32[]{:T(128)} %constant.153.clone.1, s32[]{:T(128)} %constant.153.clone.1) | dynamic-update-slice | bytes 1048580 | tf_op jit(solution)/shard_map/scatter-add | solution.py:188
  226.9 4.9 %scatter-add.29 = f32[2,2,128,512]{3,0,2,1:T(2,128)S(1)} dynamic-update-slice(f32[2,2,128,512]{3,0,2,1:T(2,128)S(1)} %scatter-add.26, f32[1,2,128,512]{3,0,2,1:T(1,128)S(1)} %slice_add_fusion.2, s32[]{:T(128)} %constant.153.clone.1, s32[]{:T(128)} %constant.153.clone.1, s32[]{:T(128)} %constant.153.clone.1, s32[]{:T(128)} %constant.153.clone.1) | dynamic-update-slice | bytes 1048580 | tf_op jit(solution)/shard_map/scatter-add | solution.py:189
  231.8 1.4 fusion.34
  234.3 46.4 %reduce-scatter.2.cloned.1.call-done = f32[16,512]{1,0:T(8,128)} async-done(((f32[512,512]{1,0:T(8,128)}), f32[16,512]{1,0:T(8,128)}) %reduce-scatter.2.cloned.1.call-update) | async-done | bytes 32784 | tf_op jit(solution)/shard_map/reduce_scatter | solution.py:198
  280.6 1.3 scatter_fusion
  281.9 159.5 %all-reduce.4.cloned.1.call-done = (f32[512,512]{1,0:T(8,128)}, f32[512,512]{1,0:T(8,128)}, f32[512,512]{1,0:T(8,128)}, f32[512,512]{0,1:T(8,128)}, f32[512,512]{1,0:T(8,128)}, /*index=5*/f32[512,512]{1,0:T(8,128)}) async-done(((f32[512,512]{1,0:T(8,128)}, f32[512,512]{1,0:T(8,128)}, f32[512,512]{1,0:T(8,128)}, f32[512,512]{0,1:T(8,128)}, f32[512,512]{1,0:T(8,128)}, /*index=5*/f32[512,512]{1,0:T(8,128)}), ...) | async-done | bytes 6291472 | tf_op jit(solution)/shard_map/psum | solution.py:208
  441.5 2.6 copy.35
  444.1 2.4 copy.72
  446.5 1.0 copy.73
  447.4 1.0 copy.74
  448.4 1.0 copy.75
  449.4 1.0 copy.76
  (144 shorter events, 9.3 us)
Async XLA Ops:
  7.2 104.3 %copy-start = (bf16[512,512]{1,0:T(8,128)(2,1)S(1)}, bf16[512,512]{1,0:T(8,128)(2,1)}, u32[]{:S(2)}) copy-start(bf16[512,512]{1,0:T(8,128)(2,1)} %param.29) | copy-start | bytes 1572868
  7.2 15.2 %copy-start.34 = (s32[1,1,12]{2,1,0:T(1,128)S(1)}, s32[1,1,12]{2,1,0:T(1,128)}, u32[]{:S(2)}) copy-start(s32[1,1,12]{2,1,0:T(1,128)} %param.36) | copy-start | bytes 148
  7.2 15.3 %copy-start.33 = (s32[1,1,12]{2,1,0:T(1,128)S(1)}, s32[1,1,12]{2,1,0:T(1,128)}, u32[]{:S(2)}) copy-start(s32[1,1,12]{2,1,0:T(1,128)} %param.37) | copy-start | bytes 148
  7.2 15.3 %copy-start.28 = (s32[1,1,512]{2,1,0:T(1,128)S(1)}, s32[1,1,512]{2,1,0:T(1,128)}, u32[]{:S(2)}) copy-start(s32[1,1,512]{2,1,0:T(1,128)} %param.40) | copy-start | bytes 6148
  7.2 15.4 %copy-start.30 = (s32[1,1,12,128]{3,1,2,0:T(1,128)S(1)}, s32[1,1,12,128]{3,1,2,0:T(1,128)}, u32[]{:S(2)}) copy-start(s32[1,1,12,128]{3,1,2,0:T(1,128)} %param.39) | copy-start | bytes 18436
  7.2 84.2 %copy-start.29 = (s32[1,1,512]{2,1,0:T(1,128)S(1)}, s32[1,1,512]{2,1,0:T(1,128)}, u32[]{:S(2)}) copy-start(s32[1,1,512]{2,1,0:T(1,128)} %param.41) | copy-start | bytes 6148
  7.2 273.4 %reduce-scatter.2.cloned.1.call-start = ((), (), s32[]{:S(2)}) async-start(), calls=%async_computation.1 | async-start | bytes 1081344 | tf_op jit(solution)/shard_map/reduce_scatter | solution.py:198
  8.6 84.0 %copy-start.5 = (f32[2,2,128,512]{3,2,1,0:T(8,128)S(1)}, f32[2,2,128,512]{3,2,1,0:T(8,128)}, u32[]{:S(2)}) copy-start(f32[2,2,128,512]{3,2,1,0:T(8,128)} %param.27) | copy-start | bytes 3145732
  9.5 93.4 %collective-permute-start.1 = (bf16[1,2,128,512]{3,2,1,0:T(8,128)(2,1)}, bf16[1,2,128,512]{3,2,1,0:T(8,128)(2,1)}, u32[]{:S(2)}, u32[]{:S(2)}) collective-permute-start(bf16[1,2,128,512]{3,2,1,0:T(8,128)(2,1)} %get-tuple-element.90), channel_id=1, source_target_pairs={{2,0},{4,2},{6,4},{8,6},{10,8},{12,10},{14,12},{16,14},{18,16},{20... | collective-permute-start | bytes 786440 | tf_op jit(solution)/shard_map/ppermute | solution.py:30
  14.9 86.3 %collective-permute-start = (bf16[1,2,128,512]{3,2,1,0:T(8,128)(2,1)}, bf16[1,2,128,512]{3,2,1,0:T(8,128)(2,1)}, u32[]{:S(2)}, u32[]{:S(2)}) collective-permute-start(bf16[1,2,128,512]{3,2,1,0:T(8,128)(2,1)} %get-tuple-element.91), channel_id=1, source_target_pairs={{0,2},{2,4},{4,6},{6,8},{8,10},{10,12},{12,14},{14,16},{16,18},{18... | collective-permute-start | bytes 786440 | tf_op jit(solution)/shard_map/ppermute | solution.py:27
  15.8 77.8 %copy-start.9 = (bf16[512,512]{1,0:T(8,128)(2,1)S(1)}, bf16[512,512]{1,0:T(8,128)(2,1)}, u32[]{:S(2)}) copy-start(bf16[512,512]{1,0:T(8,128)(2,1)} %param.32) | copy-start | bytes 1572868
  15.8 90.5 %collective-permute-start.3 = (bf16[2,1,128,512]{3,2,1,0:T(8,128)(2,1)}, bf16[2,1,128,512]{3,2,1,0:T(8,128)(2,1)S(1)}, u32[]{:S(2)}, u32[]{:S(2)}) collective-permute-start(bf16[2,1,128,512]{3,2,1,0:T(8,128)(2,1)} %get-tuple-element.88), channel_id=1, source_target_pairs={{1,0},{3,2},{5,4},{7,6},{9,8},{11,10},{13,12},{15,14},{17,16},{19,... | collective-permute-start | bytes 786440 | tf_op jit(solution)/shard_map/ppermute | solution.py:30
  17.2 87.4 %collective-permute-start.2 = (bf16[2,1,128,512]{3,2,1,0:T(8,128)(2,1)}, bf16[2,1,128,512]{3,2,1,0:T(8,128)(2,1)}, u32[]{:S(2)}, u32[]{:S(2)}) collective-permute-start(bf16[2,1,128,512]{3,2,1,0:T(8,128)(2,1)} %get-tuple-element.89), channel_id=1, source_target_pairs={{0,1},{2,3},{4,5},{6,7},{8,9},{10,11},{12,13},{14,15},{16,17},{18,... | collective-permute-start | bytes 786440 | tf_op jit(solution)/shard_map/ppermute | solution.py:27
  98.6 2.6 copy-start.31
  109.0 1.0 copy-start.26
  109.0 1.2 copy-start.37
  109.7 1.8 copy-start.14
  110.2 1.4 copy-start.12
  110.2 1.4 copy-start.39
  110.2 1.5 copy-start.40
  111.8 4.5 copy-start.36
  116.3 1.4 copy-start.46
  122.6 1.2 copy-start.7
  122.6 1.3 copy-start.8
  122.6 1.3 copy-start.32
  123.9 1.0 copy-start.24
  123.9 1.2 copy-start.35
  125.1 1.0 copy-start.22
  126.1 24.5 %copy-start.2 = (bf16[512,512]{1,0:T(8,128)(2,1)}, bf16[512,512]{1,0:T(8,128)(2,1)S(1)}, u32[]{:S(2)}) copy-start(bf16[512,512]{1,0:T(8,128)(2,1)S(1)} %get-tuple-element.101) | copy-start | bytes 1572868
  128.5 4.0 copy-start.42
  132.5 5.8 %copy-start.16 = (bf16[12,128,512]{2,1,0:T(8,128)(2,1)}, bf16[12,128,512]{2,1,0:T(8,128)(2,1)S(1)}, u32[]{:S(2)}) copy-start(bf16[12,128,512]{2,1,0:T(8,128)(2,1)S(1)} %convolution_convert_fusion.3) | copy-start | bytes 4718596
  132.5 5.8 %copy-start.38 = (bf16[512,512]{1,0:T(8,128)(2,1)S(1)}, bf16[512,512]{1,0:T(8,128)(2,1)}, u32[]{:S(2)}) copy-start(bf16[512,512]{1,0:T(8,128)(2,1)} %param.28) | copy-start | bytes 1572868
  138.3 1.3 copy-start.44
  139.6 2.6 copy-start.4
  147.7 4.4 copy-start.23
  147.7 4.3 copy-start.25
  147.7 293.8 %all-reduce.4.cloned.1.call-start = ((), (), s32[]{:S(2)}) async-start(), calls=%async_computation.2 | async-start | bytes 12582912 | tf_op jit(solution)/shard_map/psum | solution.py:208
  152.1 1.5 slice-start
  153.6 1.6 copy-start.17
  153.6 1.6 copy-start.43
  153.6 2.2 copy-start.47
  155.8 2.2 copy-start.13
  155.8 2.2 copy-start.41
  155.8 2.3 copy-start.45
  158.0 2.3 copy-start.15
  158.0 2.3 copy-start.27
  174.2 46.8 %collective-permute-start.4 = (f32[2,128,512]{2,1,0:T(8,128)}, f32[2,128,512]{2,1,0:T(8,128)S(1)}, u32[]{:S(2)}, u32[]{:S(2)}) collective-permute-start(f32[2,128,512]{2,1,0:T(8,128)} %copy.41), channel_id=1, source_target_pairs={{0,30},{2,0},{4,2},{6,4},{8,6},{10,8},{12,10},{14,12},{16,14},{18,... | collective-permute-start | bytes 1572872 | tf_op jit(solution)/shard_map/ppermute | solution.py:11
  174.2 52.1 %collective-permute-start.5 = (f32[2,128,512]{2,1,0:T(8,128)S(1)}, f32[2,128,512]{2,1,0:T(8,128)S(1)}, u32[]{:S(2)}, u32[]{:S(2)}) collective-permute-start(f32[2,128,512]{2,1,0:T(8,128)S(1)} %copy.42), channel_id=1, source_target_pairs={{0,2},{2,4},{4,6},{6,8},{8,10},{10,12},{12,14},{14,16},{16,18},{18... | collective-permute-start | bytes 1572872 | tf_op jit(solution)/shard_map/ppermute | solution.py:11
  176.1 57.1 %collective-permute-start.7 = (bf16[2,128,512]{2,0,1:T(2,128)(2,1)}, bf16[2,128,512]{2,0,1:T(2,128)(2,1)S(1)}, u32[]{:S(2)}, u32[]{:S(2)}) collective-permute-start(bf16[2,128,512]{2,0,1:T(2,128)(2,1)} %get-tuple-element.86), channel_id=1, source_target_pairs={{0,1},{2,3},{4,5},{6,7},{8,9},{10,11},{12,13},{14,15},{16,17},{18,... | collective-permute-start | bytes 786440 | tf_op jit(solution)/shard_map/ppermute | solution.py:17
  177.7 54.1 %collective-permute-start.6 = (bf16[2,128,512]{2,0,1:T(2,128)(2,1)}, bf16[2,128,512]{2,0,1:T(2,128)(2,1)}, u32[]{:S(2)}, u32[]{:S(2)}) collective-permute-start(bf16[2,128,512]{2,0,1:T(2,128)(2,1)} %get-tuple-element.87), channel_id=1, source_target_pairs={{1,0},{3,2},{5,4},{7,6},{9,8},{11,10},{13,12},{15,14},{17,16},{19,... | collective-permute-start | bytes 786440 | tf_op jit(solution)/shard_map/ppermute | solution.py:17
  231.8 2.0 copy-start.3
  231.8 2.0 copy-start.6
  231.8 2.0 copy-start.10
  281.9 164.5 %copy-start.11 = (f32[512,512]{1,0:T(8,128)}, f32[512,512]{1,0:T(8,128)S(1)}, u32[]{:S(2)}) copy-start(f32[512,512]{1,0:T(8,128)S(1)} %scatter_fusion) | copy-start | bytes 3145732
  441.5 5.0 %copy-start.21 = (f32[512,512]{1,0:T(8,128)S(1)}, f32[512,512]{1,0:T(8,128)}, u32[]{:S(2)}) copy-start(f32[512,512]{1,0:T(8,128)} %get-tuple-element.104) | copy-start | bytes 3145732
  444.1 3.3 copy-start.20
  446.5 2.0 copy-start.19
  447.4 1.9 copy-start.18
  447.4 2.9 copy-start.1
Sparse Core Ops, SparseCore 0:
  147.8 132.7 reduce-scatter.1
  287.6 153.8 all-reduce.3
where the time goes:
time: 465 us; the launch traced here: 458 us
  waiting for transfers between devices  206 us (44%)
  blocking collectives  108 us (23%)
  matrix products  55.9 us (12%)
  local copies, waits for them, and re-layouts  45.1 us (10%)
  starting transfers between devices  15.8 us (3%)
  between operations  15.2 us (3%)
  other arithmetic  11.3 us (2%)
    psum x1, waiting for transfers between devices, body(): lax.psum((d_src, d_dst, d_bedge, d_msg, d_self, d_agg, d_bnode, d_out), (...  160 us
    all_gather x1, blocking collectives, body(): piece = lax.all_gather(coarse_rows, ('px', 'py'), axis=0, tiled=True)  68.7 us
    reduce_scatter x1, waiting for transfers between devices, body(): lax.psum_scatter(jax.ops.segment_sum(long_grad, segment, num_segments=cou...  46.4 us
    psum x1, blocking collectives, body(): lax.psum((d_src, d_dst, d_bedge, d_msg, d_self, d_agg, d_bnode, d_out), (...  39.5 us
    dot_general x19, matrix products, product(): return jnp.dot(left, right, preferred_element_type=jnp.float32)  33 us
    unnamed x110, local copies, waits for them, and re-layouts  18.8 us
  transfers between devices with their start and end apart: 10, of which 2 were waited for; matrix products, arithmetic and copies ran while one was open for 13% of the time, Pallas kernels for 0%

commit v1 on v0

v1 whole, which is shorter than its diff:
```python
import functools

import jax
import jax.numpy as jnp
from jax import lax
from jax.experimental import pallas as pl
from jax.experimental.pallas import tpu as pltpu
from jax.sharding import PartitionSpec as P

C_DEV = 16
GROUP = 4
LANES = 128
MESH = pl.DeviceIdType.MESH
F32 = jnp.float32
BF16 = jnp.bfloat16


def bits_of(size):
    return size.bit_length() - 1


def step_list(n_px, n_py, px, py):
    core = px % 2
    px_bits = list(range(1, bits_of(n_px)))
    py_bits = list(range(bits_of(n_py)))

    def px_step(bit):
        mine = (px // (1 << bit)) % 2
        return mine, (1 - 2 * mine) * (1 << bit)

    def py_step(bit):
        mine = (py // (1 << bit)) % 2
        return mine, (1 - 2 * mine) * (1 << bit)

    steps = []
    mine, move = px_step(0)
    steps.append((mine, px + move, py))
    while px_bits and py_bits:
        mine_x, move_x = px_step(px_bits.pop(0))
        mine_y, move_y = py_step(py_bits.pop(0))
        for pick in (core, 1 - core):
            other = 1 - pick
            steps.append(
                (other * mine_x + pick * mine_y, px + other * move_x, py + pick * move_y)
            )
    for bit in px_bits:
        mine, move = px_step(bit)
        steps.append((mine, px + move, py))
    for bit in py_bits:
        mine, move = py_step(bit)
        steps.append((mine, px, py + move))
    return steps


def position_of(n_px, n_py, px, py):
    place = 0
    for mine, _, _ in step_list(n_px, n_py, px, py):
        place = place * 2 + mine
    return place


def greet(partners, edges, beside):
    barrier = pltpu.get_barrier_semaphore()
    for device in partners:
        pl.semaphore_signal(barrier, inc=1, device_id=device, device_id_type=MESH)
    for condition, device in edges:

        @pl.when(condition)
        def _(device=device):
            pl.semaphore_signal(barrier, inc=1, device_id=device, device_id_type=MESH)

    pl.semaphore_wait(barrier, len(partners) + beside)


def spread_kernel(n_px, n_py, own, coarse, rim, table, send, recv, rim_send, rim_recv):
    px, py = lax.axis_index("px"), lax.axis_index("py")
    rows_x, rows_y = own.shape[:2]
    steps = step_list(n_px, n_py, px, py)
    above, below = (lax.rem(px + n_px - 1, n_px), py), (lax.rem(px + 1, n_px), py)
    before, after = (px, py - 1), (px, py + 1)
    has_before, has_after = py > 0, py < n_py - 1
    beside = (py + n_py - 1) // n_py + (2 * n_py - 2 - py) // n_py
    greet(
        [(a, b) for _, a, b in steps] + [above, below],
        [(has_before, before), (has_after, after)],
        beside,
    )

    def rim_copy(which, source, start, count, device):
        return pltpu.make_async_remote_copy(
            src_ref=source,
            dst_ref=rim.at[pl.ds(start, count)],
            send_sem=rim_send.at[which],
            recv_sem=rim_recv.at[which],
            device_id=device,
            device_id_type=MESH,
        )

    down = rim_copy(0, own.at[rows_x - 1], 0, rows_y, below)
    up = rim_copy(1, own.at[0], rows_y, rows_y, above)
    right = rim_copy(2, own.at[:, rows_y - 1], 2 * rows_y, rows_x, after)
    left = rim_copy(3, own.at[:, 0], 2 * rows_y + rows_x, rows_x, before)
    chunk = coarse.shape[0]
    base = position_of(n_px, n_py, px, py)
    table[pl.ds(pl.multiple_of(base * chunk, chunk), chunk), :] = coarse[...]
    for k, (mine, a, b) in enumerate(reversed(steps)):
        if k == 0:
            source = coarse
        else:
            source = table.at[pl.ds(pl.multiple_of(base * chunk, chunk), chunk << k)]
        copy = pltpu.make_async_remote_copy(
            src_ref=source,
            dst_ref=table.at[pl.ds(pl.multiple_of(base * chunk, chunk), chunk << k)],
            send_sem=send.at[k],
            recv_sem=recv.at[k],
            device_id=(a, b),
            device_id_type=MESH,
        )
        copy.start()
        if k == 0:
            down.start()
            up.start()
            pl.when(has_after)(right.start)
            pl.when(has_before)(left.start)

            @pl.when(jnp.logical_not(has_before))
            def _():
                rim[2 * rows_y : 2 * rows_y + rows_x] = jnp.zeros((rows_x,) + rim.shape[1:], BF16)

            @pl.when(jnp.logical_not(has_after))
            def _():
                rim[2 * rows_y + rows_x :] = jnp.zeros((rows_x,) + rim.shape[1:], BF16)

        copy.wait()
        base = base - mine * (1 << k)
    down.wait()
    up.wait()
    pl.when(has_after)(right.wait_send)
    pl.when(has_before)(right.wait_recv)
    pl.when(has_before)(left.wait_send)
    pl.when(has_after)(left.wait_recv)


def reduce_kernel(
    n_px, n_py, rows_x, rows_y, w_in, c_in, rim, w_out, c_out, rec,
    w_acc, w_got, c_acc, c_got, sems, c_sems, rim_sems, g_sems,
):
    px, py = lax.axis_index("px"), lax.axis_index("py")
    steps = step_list(n_px, n_py, px, py)
    count = len(steps)
    above, below = (lax.rem(px + n_px - 1, n_px), py), (lax.rem(px + 1, n_px), py)
    before, after = (px, py - 1), (px, py + 1)
    has_before, has_after = py > 0, py < n_py - 1
    beside = (py + n_py - 1) // n_py + (2 * n_py - 2 - py) // n_py
    greet(
        [(a, b) for _, a, b in steps] + [above, below],
        [(has_before, before), (has_after, after)],
        beside,
    )

    def rim_copy(which, start, size, device):
        return pltpu.make_async_remote_copy(
            src_ref=rim.at[pl.ds(start, size)],
            dst_ref=rec.at[pl.ds(start, size)],
            send_sem=rim_sems.at[0, which],
            recv_sem=rim_sems.at[1, which],
            device_id=device,
            device_id_type=MESH,
        )

    up = rim_copy(0, 0, rows_y, above)
    down = rim_copy(1, rows_y, rows_y, below)
    left = rim_copy(2, 2 * rows_y, rows_x, before)
    right = rim_copy(3, 2 * rows_y + rows_x, rows_x, after)

    def add_into(target, start, source, source_start, extra, extra_start, rows, piece):
        @pl.loop(0, rows // piece)
        def _(i):
            shift = i * piece
            first = source[pl.ds(pl.multiple_of(source_start + shift, 16), piece), :].astype(F32)
            second = extra[pl.ds(pl.multiple_of(extra_start + shift, 16), piece), :].astype(F32)
            target[pl.ds(pl.multiple_of(start + shift, 16), piece), :] = (first + second).astype(BF16)

    w_last = w_in.shape[0] >> count
    c_last = c_in.shape[0] >> count
    w_off, c_off = 0, 0
    got = 0
    c_at = 0
    offsets = []
    for s, (mine, a, b) in enumerate(steps):
        w_half = w_in.shape[0] >> (s + 1)
        c_half = c_in.shape[0] >> (s + 1)
        w_from, c_from = (w_in, c_in) if s == 0 else (w_acc, c_acc)
        w_keep, w_send = w_off + mine * w_half, w_off + (1 - mine) * w_half
        c_keep, c_send = c_off + mine * c_half, c_off + (1 - mine) * c_half
        w_copy = pltpu.make_async_remote_copy(
            src_ref=w_from.at[pl.ds(pl.multiple_of(w_send, 16), w_half)],
            dst_ref=w_got.at[pl.ds(got, w_half)],
            send_sem=sems.at[0, s],
            recv_sem=sems.at[1, s],
            device_id=(a, b),
            device_id_type=MESH,
        )
        c_copy = pltpu.make_async_remote_copy(
            src_ref=c_from.at[pl.ds(pl.multiple_of(c_send, 16), c_half)],
            dst_ref=c_got.at[pl.ds(c_at, c_half)],
            send_sem=c_sems.at[0, s],
            recv_sem=c_sems.at[1, s],
            device_id=(a, b),
            device_id_type=MESH,
        )
        c_copy.start()
        w_copy.start()
        if s == 1:
            up.start()
            down.start()
            pl.when(has_before)(left.start)
            pl.when(has_after)(right.start)

            @pl.when(jnp.logical_not(has_after))
            def _():
                rec[2 * rows_y : 2 * rows_y + rows_x] = jnp.zeros((rows_x,) + rec.shape[1:], BF16)

            @pl.when(jnp.logical_not(has_before))
            def _():
                rec[2 * rows_y + rows_x :] = jnp.zeros((rows_x,) + rec.shape[1:], BF16)

        final = s == count - 1
        c_copy.wait()
        if final:
            c_out[...] = (
                c_acc[pl.ds(pl.multiple_of(c_keep, 16), c_last), :].astype(F32)
                + c_got[pl.ds(c_at, c_last), :].astype(F32)
            ).astype(BF16)
        else:
            add_into(c_acc, c_keep, c_from, c_keep, c_got, c_at, c_half, c_last)
        w_copy.wait()
        add_into(w_out if final else w_acc, w_keep, w_from, w_keep, w_got, got, w_half, w_last)
        got += w_half
        c_at += c_half
        w_off, c_off = w_keep, c_keep
        offsets.append(w_keep)
    for k, (mine, a, b) in enumerate(reversed(steps)):
        s = count - 1 - k
        region = w_out.at[pl.ds(pl.multiple_of(offsets[s], 16), w_in.shape[0] >> (s + 1))]
        copy = pltpu.make_async_remote_copy(
            src_ref=region,
            dst_ref=region,
            send_sem=g_sems.at[0, k],
            recv_sem=g_sems.at[1, k],
            device_id=(a, b),
            device_id_type=MESH,
        )
        copy.start()
        copy.wait()
    up.wait()
    down.wait()
    pl.when(has_before)(left.wait_send)
    pl.when(has_after)(left.wait_recv)
    pl.when(has_after)(right.wait_send)
    pl.when(has_before)(right.wait_recv)


def dot(left, right):
    return jnp.dot(left, right, preferred_element_type=F32)


def dot_t(left, right):
    return lax.dot_general(left, right, (((0,), (0,)), ((), ())), preferred_element_type=F32)


def dot_nt(left, right):
    return lax.dot_general(left, right, (((1,), (1,)), ((), ())), preferred_element_type=F32)


def silu_and_slope(value):
    sigma = jax.nn.sigmoid(value)
    return value * sigma, sigma * (1.0 + value * (1.0 - sigma))


def local_kernel(
    src_block, dst_block, own, rim, coarse, cot, w_src, w_dst, b_edge, w_msg, w_self, w_agg,
    b_node, w_out, src_idx, dst_idx, long_src, long_dst,
    base, g_own, g_rim, g_coarse, weights,
    table, sender, pre, act_sum, g_dst, g_table, half, d_src, d_bias,
):
    inner, block, width = own.shape
    rows = inner * block
    tiles = src_idx.shape[0]
    long_count = long_src.shape[1]
    span = GROUP * block
    table[:inner] = own[...]
    table[inner:] = rim[...]
    g_table[...] = jnp.zeros_like(g_table)
    g_dst[...] = jnp.zeros_like(g_dst)
    act_sum[...] = jnp.zeros_like(act_sum)
    d_src[...] = jnp.zeros_like(d_src)
    d_bias[...] = jnp.zeros_like(d_bias)
    own_rows = own[...].reshape(rows, width)
    half[...] = dot(own_rows, w_dst[...]).astype(BF16).reshape(inner, block, width)

    def hot(index, nodes):
        count = index.shape[1]
        return (lax.broadcasted_iota(jnp.int32, (nodes, count), 0) == index).astype(BF16)

    @pl.loop(0, tiles // GROUP)
    def _(g):
        first = pl.multiple_of(g * span, span)
        for j in range(GROUP):
            t = g * GROUP + j
            at = pl.ds(pl.multiple_of(first + j * block, block), block)
            sender[at, :] = dot_t(hot(src_idx[t], block), table[src_block[t]]).astype(BF16)
            pre[at, :] = dot_t(hot(dst_idx[t], block), half[dst_block[t]])
        at = pl.ds(first, span)
        value = dot(sender[at, :], w_src[...]) + pre[at, :] + b_edge[...]
        pre[at, :] = value
        act = (value * jax.nn.sigmoid(value)).astype(BF16)
        for j in range(GROUP):
            t = g * GROUP + j
            act_sum[dst_block[t]] += dot(
                hot(dst_idx[t], block), act[j * block : (j + 1) * block]
            )

    fine = tiles * block
    long_at = slice(fine, fine + long_count)
    long_hot = hot(long_dst[...], rows)
    sender[long_at, :] = dot_t(hot(long_src[...], coarse.shape[0]), coarse[...]).astype(BF16)
    value = (
        dot(sender[long_at, :], w_src[...])
        + dot_t(long_hot, half[...].reshape(rows, width))
        + b_edge[...]
    )
    pre[long_at, :] = value
    act = (value * jax.nn.sigmoid(value)).astype(BF16)
    acts = (act_sum[...].reshape(rows, width) + dot(long_hot, act)).astype(BF16)
    incoming = dot(acts, w_msg[...]).astype(BF16)
    node_pre = dot(own_rows, w_self[...]) + dot(incoming, w_agg[...]) + b_node[...]
    node_silu, node_slope = silu_and_slope(node_pre)
    cot_rows = cot[...].reshape(rows, width)
    cot_b = cot_rows.astype(BF16)

    def put(which, value):
        value = value.astype(BF16)
        for j in range(width // LANES):
            start = (which * (width // LANES) + j) * width
            weights[start : start + width, :] = value[:, j * LANES : (j + 1) * LANES]

    put(5, dot_t(node_silu.astype(BF16), cot_b))
    g_node = (dot_nt(cot_b, w_out[...]) * node_slope).astype(BF16)
    put(3, dot_t(own_rows, g_node))
    put(4, dot_t(incoming, g_node))
    d_node = jnp.sum(g_node.astype(F32), axis=0, keepdims=True)
    g_incoming = dot_nt(g_node, w_agg[...]).astype(BF16)
    put(2, dot_t(acts, g_incoming))
    base[...] = (cot_rows + dot_nt(g_node, w_self[...])).reshape(inner, block, width)
    half[...] = dot_nt(g_incoming, w_msg[...]).astype(BF16).reshape(inner, block, width)

    @pl.loop(0, tiles // GROUP)
    def _(g):
        first = pl.multiple_of(g * span, span)
        for j in range(GROUP):
            t = g * GROUP + j
            at = pl.ds(pl.multiple_of(first + j * block, block), block)
            dst_hot = hot(dst_idx[t], block)
            _, slope = silu_and_slope(pre[at, :])
            g_pre = (dot_t(dst_hot, half[dst_block[t]]) * slope).astype(BF16)
            pre[at, :] = g_pre.astype(F32)
            g_dst[dst_block[t]] += dot(dst_hot, g_pre)
            g_table[src_block[t]] += dot(hot(src_idx[t], block), g_pre)
        at = pl.ds(first, span)
        whole = pre[at, :]
        d_src[...] += dot_t(sender[at, :], whole.astype(BF16))
        d_bias[...] += jnp.sum(whole, axis=0, keepdims=True)

    _, slope = silu_and_slope(pre[long_at, :])
    long_hot = hot(long_dst[...], rows)
    g_pre = (dot_t(long_hot, half[...].reshape(rows, width)) * slope).astype(BF16)
    g_coarse[...] = dot(hot(long_src[...], coarse.shape[0]), g_pre).astype(BF16)
    put(0, d_src[...] + dot_t(sender[long_at, :], g_pre))
    d_edge = d_bias[...] + jnp.sum(g_pre.astype(F32), axis=0, keepdims=True)
    g_recv = (g_dst[...].reshape(rows, width) + dot(long_hot, g_pre)).astype(BF16)
    put(1, dot_t(own_rows, g_recv))
    base[...] += dot_nt(g_recv, w_dst[...]).reshape(inner, block, width)
    g_own[...] = g_table[:inner]
    g_rim[...] = g_table[inner:].astype(BF16)
    start = 6 * width * (width // LANES)
    tail = weights.shape[0] - start
    weights[start:, :] = jnp.zeros((tail, LANES), BF16)
    parts = [v[:, j * LANES : (j + 1) * LANES] for v in (d_edge, d_node) for j in range(width // LANES)]
    parts.append(jnp.zeros((16 - len(parts), LANES), F32))
    weights[start : start + 16, :] = jnp.concatenate(parts, axis=0).astype(BF16)


def finish_kernel(
    rows_x, rows_y, base, g_own, rec, c_sum, w_src, weights,
    grad, d_src, d_dst, b_edge, d_msg, d_self, d_agg, b_node, d_out, total,
):
    inner, block, width = base.shape
    rows = inner * block
    count = c_sum.shape[0]
    stride = rows // count
    node = lax.broadcasted_iota(jnp.int32, (rows, count), 0)
    place = lax.broadcasted_iota(jnp.int32, (rows, count), 1) * stride
    pick = (node == place).astype(BF16)
    total[...] = g_own[...] + dot(pick, c_sum[...]).reshape(inner, block, width)
    for c in range(rows_y):
        total[(rows_x - 1) * rows_y + c] += rec[c].astype(F32)
        total[c] += rec[rows_y + c].astype(F32)
    for r in range(rows_x):
        total[r * rows_y + rows_y - 1] += rec[2 * rows_y + r].astype(F32)
        total[r * rows_y] += rec[2 * rows_y + rows_x + r].astype(F32)
    sent = total[...].reshape(rows, width).astype(BF16)
    grad[...] = base[...] + dot_nt(sent, w_src[...]).reshape(inner, block, width)
    cols = width // LANES
    for which, ref in enumerate((d_src, d_dst, d_msg, d_self, d_agg, d_out)):
        for j in range(cols):
            start = (which * cols + j) * width
            ref[:, j * LANES : (j + 1) * LANES] = weights[start : start + width, :].astype(F32)
    start = 6 * width * cols
    bias = weights[start : start + 16, :].astype(F32)
    for j in range(cols):
        b_edge[:, j * LANES : (j + 1) * LANES] = bias[j : j + 1]
        b_node[:, j * LANES : (j + 1) * LANES] = bias[cols + j : cols + j + 1]


def vmem(count):
    return [pl.BlockSpec(memory_space=pltpu.VMEM)] * count


def body(
    n_px, n_py, latents, cotangent, w_src, w_dst, b_edge, w_msg, w_self, w_agg, b_node, w_out,
    src_block, dst_block, src_node, dst_node, long_src, long_dst,
):
    rows_x, rows_y, block, width = latents.shape
    inner = rows_x * rows_y
    nodes = inner * block
    rims = 2 * (rows_x + rows_y)
    tiles = src_block.shape[-1]
    long_count = long_src.shape[-1]
    edges = tiles * block + long_count
    devices = n_px * n_py
    stride = nodes // C_DEV
    steps = bits_of(n_px) + bits_of(n_py)
    coarse_count = C_DEV * devices
    exact = 6 * width * width // LANES + 16
    unit = 16 * devices
    w_rows = -(-exact // unit) * unit
    shape = jax.ShapeDtypeStruct
    dma = pltpu.SemaphoreType.DMA

    rounded = latents.astype(BF16)
    coarse_rows = latents.reshape(nodes, width)[::stride].astype(BF16)
    rim, coarse = pl.pallas_call(
        functools.partial(spread_kernel, n_px, n_py),
        out_shape=(shape((rims, block, width), BF16), shape((coarse_count, width), BF16)),
        in_specs=vmem(2),
        out_specs=tuple(vmem(2)),
        scratch_shapes=[dma((steps,)), dma((steps,)), dma((4,)), dma((4,))],
        compiler_params=pltpu.CompilerParams(collective_id=0, has_side_effects=True),
        name="spread",
    )(rounded, coarse_rows)

    owner = long_src.reshape(1, long_count) // C_DEV
    place = position_of(n_px, n_py, owner // n_py, owner % n_py)
    long_place = place * C_DEV + long_src.reshape(1, long_count) % C_DEV

    smem = [pl.BlockSpec(memory_space=pltpu.SMEM)] * 2
    base, g_own, g_rim, g_coarse, weights = pl.pallas_call(
        local_kernel,
        out_shape=(
            shape((inner, block, width), F32),
            shape((inner, block, width), F32),
            shape((rims, block, width), BF16),
            shape((coarse_count, width), BF16),
            shape((w_rows, LANES), BF16),
        ),
        in_specs=smem + vmem(16),
        out_specs=tuple(vmem(5)),
        scratch_shapes=[
            pltpu.VMEM((inner + rims, block, width), BF16),
            pltpu.VMEM((edges, width), BF16),
            pltpu.VMEM((edges, width), F32),
            pltpu.VMEM((inner, block, width), F32),
            pltpu.VMEM((inner, block, width), F32),
            pltpu.VMEM((inner + rims, block, width), F32),
            pltpu.VMEM((inner, block, width), BF16),
            pltpu.VMEM((width, width), F32),
            pltpu.VMEM((1, width), F32),
        ],
        compiler_params=pltpu.CompilerParams(vmem_limit_bytes=60 * 1024 * 1024),
        name="local",
    )(
        src_block.reshape(tiles), dst_block.reshape(tiles),
        rounded.reshape(inner, block, width), rim, coarse,
        cotangent.reshape(inner, block, width),
        w_src, w_dst, b_edge.reshape(1, width), w_msg, w_self, w_agg, b_node.reshape(1, width),
        w_out, src_node.reshape(tiles, 1, block), dst_node.reshape(tiles, 1, block),
        long_place, long_dst.reshape(1, long_count),
    )

    w_sum, c_sum, rec = pl.pallas_call(
        functools.partial(reduce_kernel, n_px, n_py, rows_x, rows_y),
        out_shape=(
            shape((w_rows, LANES), BF16),
            shape((C_DEV, width), BF16),
            shape((rims, block, width), BF16),
        ),
        in_specs=vmem(3),
        out_specs=tuple(vmem(3)),
        scratch_shapes=[
            pltpu.VMEM((w_rows, LANES), BF16),
            pltpu.VMEM((w_rows, LANES), BF16),
            pltpu.VMEM((coarse_count, width), BF16),
            pltpu.VMEM((coarse_count, width), BF16),
            dma((2, steps)), dma((2, steps)), dma((2, 4)), dma((2, steps)),
        ],
        compiler_params=pltpu.CompilerParams(
            collective_id=1, has_side_effects=True, vmem_limit_bytes=60 * 1024 * 1024
        ),
        name="reduce",
    )(weights, g_coarse, g_rim)

    matrix, vector = shape((width, width), F32), shape((1, width), F32)
    grad, d_src, d_dst, d_edge, d_msg, d_self, d_agg, d_node, d_out = pl.pallas_call(
        functools.partial(finish_kernel, rows_x, rows_y),
        out_shape=(
            shape((inner, block, width), F32),
            matrix, matrix, vector, matrix, matrix, matrix, vector, matrix,
        ),
        in_specs=vmem(6),
        out_specs=tuple(vmem(9)),
        scratch_shapes=[pltpu.VMEM((inner, block, width), F32)],
        compiler_params=pltpu.CompilerParams(vmem_limit_bytes=60 * 1024 * 1024),
        name="finish",
    )(base, g_own, rec, c_sum, w_src, w_sum)
    return (
        grad.reshape(latents.shape), d_src, d_dst, d_edge.reshape(width), d_msg, d_self, d_agg,
        d_node.reshape(width), d_out,
    )


def solution(mesh):
    n_px, n_py = mesh.shape["px"], mesh.shape["py"]
    part = {4: P("px", "py", None, None), 3: P("px", "py", None)}
    in_specs = (part[4], part[4]) + (P(),) * 8 + (part[3], part[3], part[4], part[4], part[3], part[3])
    out_specs = (part[4],) + (P(),) * 8
    return jax.shard_map(
        functools.partial(body, n_px, n_py),
        mesh=mesh, in_specs=in_specs, out_specs=out_specs, check_vma=False,
    )
```

time: 465 us -> 140 us (0.30); the launches traced: 458 us -> 140 us
  waiting for transfers between devices: 206 us -> 0 us
  Pallas kernels: 0 us -> 136 us
  blocking collectives: 108 us -> 0 us
  matrix products: 55.9 us -> 0 us
  local copies, waits for them, and re-layouts: 45.1 us -> 0.79 us
  starting transfers between devices: 15.8 us -> 0 us
  between operations: 15.2 us -> 0.67 us
  other arithmetic: 11.3 us -> 2.65 us
    psum x1 -> x0, waiting for transfers between devices: 160 us -> none  [body(): lax.psum((d_src, d_dst, d_bedge, d_msg, d_self, d_agg, d_bnode, d_out), (...]
    pallas_call x0 -> x4, Pallas kernels: none -> 136 us  [the longest x1 83.8 us: body(): pl.pallas_call(functools.partial(reduce_kernel, n_px, n_py, rows_x, rows_...]
    all_gather x1 -> x0, blocking collectives: 68.7 us -> none  [body(): piece = lax.all_gather(coarse_rows, ('px', 'py'), axis=0, tiled=True)]
    dot_general x30 -> x0, matrix products: 55.9 us -> none  [the longest x19 33 us: product(): return jnp.dot(left, right, preferred_element_type=jnp.float32)]
    reduce_scatter x1 -> x0, waiting for transfers between devices: 46.4 us -> none  [body(): lax.psum_scatter(jax.ops.segment_sum(long_grad, segment, num_segments=cou...]
    psum x1 -> x0, blocking collectives: 39.5 us -> none  [body(): lax.psum((d_src, d_dst, d_bedge, d_msg, d_self, d_agg, d_bnode, d_out), (...]
    unnamed x110 -> x2, local copies, waits for them, and re-layouts: 18.8 us -> 0.06 us
    ppermute x8 -> x0, starting transfers between devices: 15.8 us -> none  [the longest x2 6.86 us: padded(): lax.ppermute(lax.slice_in_dim(block, 0, width, axis=dim), axis, backward)]
  transfers between devices with their start and end apart: 10 -> 0, of which waited for: 2 -> 0; matrix products, arithmetic and copies ran while one was open for 13% -> 0% of each run, Pallas kernels for 0% -> 0%
where the time goes in v1:
time: 140 us
  Pallas kernels  136 us (97%)
  other arithmetic  2.65 us (2%)
    pallas_call x1, Pallas kernels, body(): pl.pallas_call(functools.partial(reduce_kernel, n_px, n_py, rows_x, rows_...  83.8 us
    pallas_call x1, Pallas kernels, body(): pl.pallas_call(functools.partial(spread_kernel, n_px, n_py), out_shape=(s...  24 us
    pallas_call x1, Pallas kernels, body(): pl.pallas_call(local_kernel, out_shape=(shape((inner, block, width), F32)...  21.1 us
    pallas_call x1, Pallas kernels, body(): pl.pallas_call(functools.partial(finish_kernel, rows_x, rows_y), out_shap...  6.74 us

profile of v1, /device:TPU:0, one launch (start us, length us, event | category | flops | bytes accessed | tf_op | source)
XLA Modules:
  0.0 139.8 jit_solution(1039964570635643171)
XLA Ops:
  0.6 1.4 fusion.2.long_src
  2.0 1.3 convert_element_type.4.own
  3.3 0.0 copy-start
  3.3 0.7 slice.4.coarse
  4.0 0.1 copy-done
  4.1 24.0 %spread.1 = (bf16[8,128,512]{2,1,0:T(8,128)(2,1)}, bf16[512,512]{1,0:T(8,128)(2,1)}) custom-call(bf16[2,2,128,512]{3,2,1,0:T(8,128)(2,1)} %copy-done, bf16[16,512]{1,0:T(8,128)(2,1)} %slice.4.coarse), custom_call_target="tpu_custom_call" | custom-call | tf_op jit(solution)/shard_map/spread/pallas_call | solution.py:453
  28.1 21.1 %local.1 = (f32[4,128,512]{2,1,0:T(8,128)}, f32[4,128,512]{2,1,0:T(8,128)}, bf16[8,128,512]{2,1,0:T(8,128)(2,1)}, bf16[512,512]{1,0:T(8,128)(2,1)}, bf16[12800,128]{1,0:T(8,128)(2,1)}) custom-call(s32[12]{0:T(128)} %bitcast.34, s32[12]{0:T(128)} %bitcast.35, bf16[4,128,512]{2,1,0:T(8,128)(2,1)} %bitcast.27, bf16[8,128,512]{2,1,0:T(8,128)(2,1)} %get-tuple-element.28.rim, ...), custom_call_target="tpu_custom_call" | custom-call | tf_op jit(solution)/shard_map/local/pallas_call | solution.py:468
  49.2 83.8 %reduce.1 = (bf16[12800,128]{1,0:T(8,128)(2,1)}, bf16[16,512]{1,0:T(8,128)(2,1)}, bf16[8,128,512]{2,1,0:T(8,128)(2,1)}) custom-call(bf16[12800,128]{1,0:T(8,128)(2,1)} %get-tuple-element.32.w_in, bf16[512,512]{1,0:T(8,128)(2,1)} %get-tuple-element.33.c_in, bf16[8,128,512]{2,1,0:T(8,128)(2,1)} %get-tuple-element.34.rim), custom_call_target="tpu_custom_call" | custom-call | tf_op jit(solution)/shard_map/reduce/pallas_call | solution.py:501
  133.0 6.7 %finish.1 = (f32[4,128,512]{2,1,0:T(8,128)}, f32[512,512]{1,0:T(8,128)}, f32[512,512]{1,0:T(8,128)}, f32[1,512]{1,0:T(1,128)}, f32[512,512]{1,0:T(8,128)}, /*ind...) custom-call(f32[4,128,512]{2,1,0:T(8,128)} %get-tuple-element.30.base, ...), custom_call_target="tpu_custom_call" | custom-call | tf_op jit(solution)/shard_map/finish/pallas_call | solution.py:524
Async XLA Ops:
  3.3 0.8 copy-start

commit v2 on v1

--- a/solution.py
+++ b/solution.py
@@ -9,6 +9,8 @@
 
 C_DEV = 16
 GROUP = 4
+CHUNKS = 4
+COARSE_DELAY = 2
 LANES = 128
 MESH = pl.DeviceIdType.MESH
 F32 = jnp.float32
@@ -143,7 +145,7 @@
 
 def reduce_kernel(
     n_px, n_py, rows_x, rows_y, w_in, c_in, rim, w_out, c_out, rec,
-    w_acc, w_got, c_acc, c_got, sems, c_sems, rim_sems, g_sems,
+    w_acc, w_got, c_acc, c_got, sems, rim_sems,
 ):
     px, py = lax.axis_index("px"), lax.axis_index("py")
     steps = step_list(n_px, n_py, px, py)
@@ -181,37 +183,69 @@
             second = extra[pl.ds(pl.multiple_of(extra_start + shift, 16), piece), :].astype(F32)
             target[pl.ds(pl.multiple_of(start + shift, 16), piece), :] = (first + second).astype(BF16)
 
-    w_last = w_in.shape[0] >> count
-    c_last = c_in.shape[0] >> count
-    w_off, c_off = 0, 0
-    got = 0
-    c_at = 0
-    offsets = []
-    for s, (mine, a, b) in enumerate(steps):
-        w_half = w_in.shape[0] >> (s + 1)
-        c_half = c_in.shape[0] >> (s + 1)
-        w_from, c_from = (w_in, c_in) if s == 0 else (w_acc, c_acc)
-        w_keep, w_send = w_off + mine * w_half, w_off + (1 - mine) * w_half
-        c_keep, c_send = c_off + mine * c_half, c_off + (1 - mine) * c_half
-        w_copy = pltpu.make_async_remote_copy(
-            src_ref=w_from.at[pl.ds(pl.multiple_of(w_send, 16), w_half)],
-            dst_ref=w_got.at[pl.ds(got, w_half)],
-            send_sem=sems.at[0, s],
-            recv_sem=sems.at[1, s],
-            device_id=(a, b),
-            device_id_type=MESH,
+    unit = 16 << count
+    units = w_in.shape[0] // unit
+    streams = []
+    start = 0
+    for c in range(CHUNKS):
+        rows = (units // CHUNKS + (1 if c < units % CHUNKS else 0)) * unit
+        if rows:
+            streams.append(
+                dict(delay=c, first=start, rows=rows, full=w_in, acc=w_acc, got=w_got, out=w_out, gather=True)
+            )
+        start += rows
+    streams.append(
+        dict(delay=COARSE_DELAY, first=0, rows=c_in.shape[0], full=c_in, acc=c_acc, got=c_got, out=c_out, gather=False)
+    )
+    for stream in streams:
+        stream.update(at=stream["first"], landing=stream["first"], kept=[])
+
+    def launch(which, stream, s):
+        if s < count:
+            mine, a, b = steps[s]
+            size = stream["rows"] >> (s + 1)
+            source = stream["full"] if s == 0 else stream["acc"]
+            away = stream["at"] + (1 - mine) * size
+            src = source.at[pl.ds(pl.multiple_of(away, 16), size)]
+            dst = stream["got"].at[pl.ds(stream["landing"], size)]
+        else:
+            _, a, b = steps[2 * count - 1 - s]
+            size = stream["rows"] >> (2 * count - s)
+            src = stream["out"].at[pl.ds(pl.multiple_of(stream["kept"][2 * count - 1 - s], 16), size)]
+            dst = src
+        stream["copy"] = pltpu.make_async_remote_copy(
+            src_ref=src, dst_ref=dst,
+            send_sem=sems.at[0, which, s], recv_sem=sems.at[1, which, s],
+            device_id=(a, b), device_id_type=MESH,
         )
-        c_copy = pltpu.make_async_remote_copy(
-            src_ref=c_from.at[pl.ds(pl.multiple_of(c_send, 16), c_half)],
-            dst_ref=c_got.at[pl.ds(c_at, c_half)],
-            send_sem=c_sems.at[0, s],
-            recv_sem=c_sems.at[1, s],
-            device_id=(a, b),
-            device_id_type=MESH,
-        )
-        c_copy.start()
-        w_copy.start()
-        if s == 1:
+        stream["copy"].start()
+
+    def settle(stream, s):
+        stream["copy"].wait()
+        if s >= count:
+            return
+        mine = steps[s][0]
+        size = stream["rows"] >> (s + 1)
+        keep = stream["at"] + mine * size
+        source = stream["full"] if s == 0 else stream["acc"]
+        final = s == count - 1
+        target = stream["out"] if final else stream["acc"]
+        to = keep if stream["gather"] or not final else 0
+        piece = stream["rows"] >> count
+        add_into(target, to, source, keep, stream["got"], stream["landing"], size, piece)
+        stream["at"] = keep
+        stream["landing"] += size
+        stream["kept"].append(keep)
+
+    for slot in range(2 * count + max(CHUNKS, COARSE_DELAY) + 1):
+        for which, stream in enumerate(streams):
+            s = slot - stream["delay"]
+            total = 2 * count if stream["gather"] else count
+            if 1 <= s <= total:
+                settle(stream, s - 1)
+            if 0 <= s < total:
+                launch(which, stream, s)
+        if slot == 0:
             up.start()
             down.start()
             pl.when(has_before)(left.start)
@@ -225,34 +259,6 @@
             def _():
                 rec[2 * rows_y + rows_x :] = jnp.zeros((rows_x,) + rec.shape[1:], BF16)
 
-        final = s == count - 1
-        c_copy.wait()
-        if final:
-            c_out[...] = (
-                c_acc[pl.ds(pl.multiple_of(c_keep, 16), c_last), :].astype(F32)
-                + c_got[pl.ds(c_at, c_last), :].astype(F32)
-            ).astype(BF16)
-        else:
-            add_into(c_acc, c_keep, c_from, c_keep, c_got, c_at, c_half, c_last)
-        w_copy.wait()
-        add_into(w_out if final else w_acc, w_keep, w_from, w_keep, w_got, got, w_half, w_last)
-        got += w_half
-        c_at += c_half
-        w_off, c_off = w_keep, c_keep
-        offsets.append(w_keep)
-    for k, (mine, a, b) in enumerate(reversed(steps)):
-        s = count - 1 - k
-        region = w_out.at[pl.ds(pl.multiple_of(offsets[s], 16), w_in.shape[0] >> (s + 1))]
-        copy = pltpu.make_async_remote_copy(
-            src_ref=region,
-            dst_ref=region,
-            send_sem=g_sems.at[0, k],
-            recv_sem=g_sems.at[1, k],
-            device_id=(a, b),
-            device_id_type=MESH,
-        )
-        copy.start()
-        copy.wait()
     up.wait()
     down.wait()
     pl.when(has_before)(left.wait_send)
@@ -512,7 +518,7 @@
             pltpu.VMEM((w_rows, LANES), BF16),
             pltpu.VMEM((coarse_count, width), BF16),
             pltpu.VMEM((coarse_count, width), BF16),
-            dma((2, steps)), dma((2, steps)), dma((2, 4)), dma((2, steps)),
+            dma((2, CHUNKS + 1, 2 * steps)), dma((2, 4)),
         ],
         compiler_params=pltpu.CompilerParams(
             collective_id=1, has_side_effects=True, vmem_limit_bytes=60 * 1024 * 1024

time: 140 us -> 120 us (0.86)
  Pallas kernels: 136 us -> 116 us
    pallas_call x1, Pallas kernels: 83.8 us -> 64 us  [body(): pl.pallas_call(functools.partial(reduce_kernel, n_px, n_py, rows_x, rows_...]
where the time goes in v2:
time: 120 us
  Pallas kernels  116 us (97%)
  other arithmetic  2.65 us (2%)
    pallas_call x1, Pallas kernels, body(): pl.pallas_call(functools.partial(reduce_kernel, n_px, n_py, rows_x, rows_...  64 us
    pallas_call x1, Pallas kernels, body(): pl.pallas_call(functools.partial(spread_kernel, n_px, n_py), out_shape=(s...  24 us
    pallas_call x1, Pallas kernels, body(): pl.pallas_call(local_kernel, out_shape=(shape((inner, block, width), F32)...  21.1 us
    pallas_call x1, Pallas kernels, body(): pl.pallas_call(functools.partial(finish_kernel, rows_x, rows_y), out_shap...  6.74 us

profile of v2, /device:TPU:0, one launch (start us, length us, event | category | flops | bytes accessed | tf_op | source)
XLA Modules:
  0.0 119.9 jit_solution(2396237442233504244)
XLA Ops:
  0.6 1.4 %fusion.2.long_src = s32[1,512]{1,0:T(1,128)} fusion(s32[1,1,512]{2,1,0:T(1,128)} %param.30), kind=kLoop, calls=%fused_computation.35 | loop fusion | flops 70656 | bytes 4096 | tf_op jit(solution)/shard_map/add | solution.py:471
  2.0 1.3 %convert_element_type.4.own = bf16[2,2,128,512]{3,2,1,0:T(8,128)(2,1)S(1)} convert(f32[2,2,128,512]{3,2,1,0:T(8,128)} %param.16) | non-fusion elementwise | flops 262144 | bytes 1572864 | tf_op jit(solution)/shard_map/convert_element_type | solution.py:457
  3.3 0.0 copy-start
  3.3 0.7 slice.4.coarse
  4.0 0.1 copy-done
  4.1 24.0 %spread.1 = (bf16[8,128,512]{2,1,0:T(8,128)(2,1)}, bf16[512,512]{1,0:T(8,128)(2,1)}) custom-call(bf16[2,2,128,512]{3,2,1,0:T(8,128)(2,1)} %copy-done, bf16[16,512]{1,0:T(8,128)(2,1)} %slice.4.coarse), custom_call_target="tpu_custom_call" | custom-call | tf_op jit(solution)/shard_map/spread/pallas_call | solution.py:459
  28.1 21.1 %local.1 = (f32[4,128,512]{2,1,0:T(8,128)}, f32[4,128,512]{2,1,0:T(8,128)}, bf16[8,128,512]{2,1,0:T(8,128)(2,1)}, bf16[512,512]{1,0:T(8,128)(2,1)}, bf16[12800,128]{1,0:T(8,128)(2,1)}) custom-call(s32[12]{0:T(128)} %bitcast.34, s32[12]{0:T(128)} %bitcast.35, bf16[4,128,512]{2,1,0:T(8,128)(2,1)} %bitcast.27, bf16[8,128,512]{2,1,0:T(8,128)(2,1)} %get-tuple-element.28.rim, ...), custom_call_target="tpu_custom_call" | custom-call | tf_op jit(solution)/shard_map/local/pallas_call | solution.py:474
  49.2 64.0 %reduce.1 = (bf16[12800,128]{1,0:T(8,128)(2,1)}, bf16[16,512]{1,0:T(8,128)(2,1)}, bf16[8,128,512]{2,1,0:T(8,128)(2,1)}) custom-call(bf16[12800,128]{1,0:T(8,128)(2,1)} %get-tuple-element.32.w_in, bf16[512,512]{1,0:T(8,128)(2,1)} %get-tuple-element.33.c_in, bf16[8,128,512]{2,1,0:T(8,128)(2,1)} %get-tuple-element.34.rim), custom_call_target="tpu_custom_call" | custom-call | tf_op jit(solution)/shard_map/reduce/pallas_call | solution.py:507
  113.1 6.7 %finish.1 = (f32[4,128,512]{2,1,0:T(8,128)}, f32[512,512]{1,0:T(8,128)}, f32[512,512]{1,0:T(8,128)}, f32[1,512]{1,0:T(1,128)}, f32[512,512]{1,0:T(8,128)}, /*ind...) custom-call(f32[4,128,512]{2,1,0:T(8,128)} %get-tuple-element.30.base, ...), custom_call_target="tpu_custom_call" | custom-call | tf_op jit(solution)/shard_map/finish/pallas_call | solution.py:530
Async XLA Ops:
  3.3 0.8 copy-start
